TPU v7x, 512 devices: a whole 4x8x8 slice. The times are simulated.
512 devices in a mesh: dp: 16 (over z, core), seq: 32 (over x, y).
Axes of the slice: x: 4, y: 8, z: 8, core: 2. Of those that a mesh axis runs over, the one named last changes fastest.
Arguments:
- inputs: bfloat16 [16, 4096, 4096], P('dp', 'seq'), may hold values from -6 to 6
- out_grads: bfloat16 [16, 4096, 14336], P('dp', 'seq'), may hold values from -6 to 6
- valid: int32 [16, 4096], P('dp', 'seq'), may hold values 0 or 1
- doc_blocks: int32 [16, 4], P('dp'), may hold values from 1 to 16, 32 in all within a row
- doc_ids: int32 [64], replicated, may hold values from 0 to 63, each once
- proj_in: bfloat16 [4096, 64], P('seq'), may hold values from -0.09375 to 0.09375
- proj_out: bfloat16 [14336, 64], P('seq'), may hold values from -0.046875 to 0.046875
- test_grads: bfloat16 [1024, 4096], P('seq'), may hold values from -192 to 192
Outputs:
- scores: float32 [64, 1024], P(None, 'seq')
Inputs may be any that keep to these rules, and one draw needn't show every extreme that they name: `doc_blocks`: each group's lengths sum to 32; the largest is 16 in every group. `doc_ids`: every document number appears once.
All inputs are finite; a program needn't handle non-finite values. No bound on the sum of `valid` on one device may be relied on, other than what follows from the above.
Results may differ from a plain program's by a relative error of at most 0.0003.
Values may be sent and summed in bfloat16 or wider, within the bound.
A program may use at most 64 MiB of HBM per device.

v0:
```python
import jax
import jax.numpy as jnp
from jax import lax
from jax.sharding import PartitionSpec as P

PROJ_OUT = 64
FEAT = 4096
BLOCK = 128
DOC_GRP = 4


def per_device(inputs, out_grads, valid, doc_blocks, doc_ids, proj_in, proj_out, test_grads):
    tokens = inputs[0]
    outgrad = out_grads[0]
    slots = tokens.shape[0]
    columns = tokens
    px = jnp.dot(
        columns,
        lax.all_gather(proj_in, "seq", axis=0, tiled=True),
        preferred_element_type=jnp.float32,
    )
    columns = outgrad
    pg = jnp.dot(
        columns,
        lax.all_gather(proj_out, "seq", axis=0, tiled=True),
        preferred_element_type=jnp.float32,
    )
    ends = jnp.cumsum(doc_blocks[0])
    position = lax.axis_index("seq") * slots + jnp.arange(slots, dtype=jnp.int32)
    blk = position // BLOCK
    owner = jnp.sum((blk[:, None] >= ends[None, :]).astype(jnp.int32), axis=1)
    onehot = (
        (owner[:, None] == jnp.arange(DOC_GRP, dtype=jnp.int32)[None, :]) & (valid[0][:, None] == 1)
    ).astype(jnp.float32)
    weighted = (onehot[:, :, None] * pg[:, None, :]).reshape(slots, DOC_GRP * PROJ_OUT)
    partial_grads = jnp.dot(weighted.T, px, precision=lax.Precision.HIGHEST).reshape(DOC_GRP, FEAT)
    ndocs = DOC_GRP * lax.axis_size("dp")
    group_grads = lax.psum(partial_grads, "seq")
    doc_grads = lax.all_gather(group_grads, "dp", axis=0, tiled=True)
    gram = jnp.dot(doc_grads, doc_grads.T, precision=lax.Precision.HIGHEST)
    cross = jnp.dot(doc_grads, test_grads.astype(jnp.float32).T, precision=lax.Precision.HIGHEST)
    damp = 0.1 * jnp.trace(gram) / ndocs
    matrix = gram / ndocs + damp * jnp.eye(ndocs, dtype=jnp.float32)
    factor = jnp.linalg.cholesky(matrix)
    middle = lax.linalg.triangular_solve(factor, cross, left_side=True, lower=True)
    solved = lax.linalg.triangular_solve(
        factor, middle, left_side=True, lower=True, transpose_a=True
    )
    placing = (doc_ids[None, :] == jnp.arange(ndocs, dtype=jnp.int32)[:, None]).astype(jnp.float32)
    return jnp.dot(placing, solved, precision=lax.Precision.HIGHEST)


def solution(mesh):
    in_specs = (
        P("dp", "seq", None),
        P("dp", "seq", None),
        P("dp", "seq"),
        P("dp", None),
        P(),
        P("seq", None),
        P("seq", None),
        P("seq", None),
    )
    out_specs = P(None, "seq")
    return jax.shard_map(
        per_device, mesh=mesh, in_specs=in_specs, out_specs=out_specs, check_vma=False
    )
```

profile of v0, /device:TPU:1, one launch (start us, length us, event | category | flops | bytes accessed | tf_op | source)
XLA Modules:
  0.0 325.9 jit_solution(14330074124522014039)
XLA Ops:
  6.5 0.0 copy-start
  6.5 0.0 all-gather.5.cloned.1.call-start
  6.5 0.7 all-gather.5.cloned.1.call-update
  7.3 0.0 all-reduce.2.cloned.1.call-start
  7.3 0.8 reduce-window.8
  8.1 0.1 convert_reduce_fusion
  8.2 41.4 %all_gather.10 = bf16[4096,64]{0,1:T(8,128)(2,1)S(1)} all-gather(bf16[128,64]{0,1:T(8,128)(2,1)} %param.13), channel_id=1, replica_groups=mesh['dp'=16,'seq'=32] {'seq'}, dimensions={0}, use_global_device_ids=true | all-gather | bytes 540672 | tf_op jit(solution)/shard_map/all_gather | solution.py:19
  49.6 0.7 compare_bitcast_fusion
  50.3 0.0 copy-done
  50.3 0.5 fusion.2
  50.8 44.7 %all-gather.5.cloned.1.call-done = bf16[32,448,64]{1,2,0:T(8,128)(2,1)} async-done(((bf16[1,448,64]{1,2,0:T(8,128)(2,1)}), bf16[32,448,64]{1,2,0:T(8,128)(2,1)}) %all-gather.5.cloned.1.call-update) | async-done | bytes 1835024 | tf_op jit(solution)/shard_map/all_gather | solution.py:25
  95.6 2.8 copy.20
  98.3 3.4 %reshape.113 = bf16[14336,64]{0,1:T(8,128)(2,1)} reshape(bf16[32,448,64]{1,0,2:T(8,128)(2,1)S(1)} %copy.20) | data formatting | bytes 3670016
  101.7 4.0 %fusion = f32[128,64]{0,1:T(8,128)S(1)} fusion(bf16[14336,64]{0,1:T(8,128)(2,1)} %reshape.113, bf16[1,128,14336]{2,1,0:T(8,128)(2,1)} %param.9), kind=kOutput, calls=%fused_computation | convolution fusion | flops 234881024 | bytes 5537792 | tf_op jit(solution)/shard_map/dot_general | solution.py:23
  105.7 0.3 fusion.15
  106.0 0.7 reshape.111
  106.7 0.0 all-reduce.2.cloned.1.call-update
  106.7 0.0 all-gather.7.cloned.1.call-start
  106.8 147.6 %all-reduce.2.cloned.1.call-done = f32[4,4096]{1,0:T(4,128)} async-done(((f32[4,4096]{1,0:T(4,128)}), f32[4,4096]{1,0:T(4,128)}) %all-reduce.2.cloned.1.call-update) | async-done | bytes 65552 | tf_op jit(solution)/shard_map/psum | solution.py:38
  254.4 0.0 all-gather.7.cloned.1.call-update
  254.4 0.0 copy-start.1
  254.4 47.1 %all-gather.7.cloned.1.call-done = f32[16,4,4096]{2,1,0:T(4,128)} async-done(((f32[1,4,4096]{2,1,0:T(4,128)}), f32[16,4,4096]{2,1,0:T(4,128)}) %all-gather.7.cloned.1.call-update) | async-done | bytes 1048592 | tf_op jit(solution)/shard_map/all_gather | solution.py:39
  301.5 1.6 reshape.115
  303.1 0.0 copy-start.2
  303.1 1.6 select_reduce_fusion.1
  304.7 0.1 copy.22
  304.8 0.1 copy.23
  305.6 5.8 %cholesky.17 = f32[64,64]{1,0:T(8,128)S(1)} custom-call(f32[64,64]{1,0:T(8,128)S(1)} %fusion.10), custom_call_target="Cholesky" | custom-call | tf_op jit(solution)/shard_map/jit(cholesky)/cholesky | solution.py:44
  311.4 0.6 compare_reduce_fusion
  312.1 0.7 fusion.4
  312.8 4.9 %custom-call.8 = f32[1,64,64]{1,2,0:T(8,128)S(1)} custom-call(f32[1,64,64]{2,1,0:T(8,128)S(1)} %fusion.4), custom_call_target="InvertDiagBlocksLowerTriangular" | custom-call | tf_op jit(solution)/shard_map/triangular_solve | solution.py:46
  317.6 0.0 copy-done.1
  317.7 0.6 fusion.16
  318.3 0.1 fusion.7
  318.4 0.2 fusion.5
  318.6 0.0 copy-done.2
  318.6 0.8 fusion.11
  (6 shorter events, 0.1 us)
Async XLA Ops:
  6.5 43.8 %copy-start = (bf16[1,128,4096]{2,1,0:T(8,128)(2,1)S(1)}, bf16[1,128,4096]{2,1,0:T(8,128)(2,1)}, u32[]{:S(2)}) copy-start(bf16[1,128,4096]{2,1,0:T(8,128)(2,1)} %param.8) | copy-start | bytes 3145732
  6.5 89.0 %all-gather.5.cloned.1.call-start = ((), (), s32[]{:S(2)}) async-start(), calls=%async_computation.1 | async-start | bytes 2162688 | tf_op jit(solution)/shard_map/all_gather | solution.py:25
  7.3 247.2 %all-reduce.2.cloned.1.call-start = ((), (), s32[]{:S(2)}) async-start(), calls=%async_computation | async-start | bytes 131072 | tf_op jit(solution)/shard_map/psum | solution.py:38
  106.7 194.8 %all-gather.7.cloned.1.call-start = ((), (), s32[]{:S(2)}) async-start(), calls=%async_computation.2 | async-start | bytes 1114112 | tf_op jit(solution)/shard_map/all_gather | solution.py:39
  254.4 63.2 %copy-start.1 = (bf16[32,4096]{1,0:T(8,128)(2,1)S(1)}, bf16[32,4096]{1,0:T(8,128)(2,1)}, u32[]{:S(2)}) copy-start(bf16[32,4096]{1,0:T(8,128)(2,1)} %param.15) | copy-start | bytes 786436
  303.1 15.5 %copy-start.2 = (s32[64]{0:T(128)S(1)}, s32[64]{0:T(128)}, u32[]{:S(2)}) copy-start(s32[64]{0:T(128)} %param.12) | copy-start | bytes 772
Sparse Core Ops, SparseCore 0:
  10.5 84.9 all-gather.4
  106.8 147.5 all-reduce.1
  256.5 44.9 all-gather.6
where the time goes:
time: 326 us
  waiting for transfers between devices  240 us (74%)
  blocking collectives  41.4 us (13%)
  between operations  13.9 us (4%)
  other arithmetic  13.7 us (4%)
  local copies, waits for them, and re-layouts  8.61 us (3%)
  matrix products  8 us (2%)
    psum x1, waiting for transfers between devices, per_device(): group_grads = lax.psum(partial_grads, 'seq')  148 us
    all_gather x1, waiting for transfers between devices, per_device(): doc_grads = lax.all_gather(group_grads, 'dp', axis=0, tiled=True)  47.1 us
    all_gather x1, waiting for transfers between devices, per_device(): lax.all_gather(proj_out, 'seq', axis=0, tiled=True)  44.7 us
    all_gather x1, blocking collectives, per_device(): lax.all_gather(proj_in, 'seq', axis=0, tiled=True)  41.4 us
  transfers between devices with their start and end apart: 3, of which 3 were waited for; matrix products, arithmetic and copies ran while one was open for 1% of the time, Pallas kernels for 0%

commit v1 on v0

--- a/solution.py
+++ b/solution.py
@@ -1,3 +1,4 @@
+import functools
 import jax
 import jax.numpy as jnp
 from jax import lax
@@ -7,6 +8,17 @@
 FEAT = 4096
 BLOCK = 128
 DOC_GRP = 4
+
+
+def ends_tell(patch, axis_name):
+    n_parts = lax.axis_size(axis_name)
+    block_now = patch
+    for idx in [[(i, i ^ j) for i in range(n_parts)] for j in (1, 2, 4, 8, 16) if j < n_parts]:
+        block_now = block_now + lax.ppermute(block_now, axis_name, idx)
+    return block_now
+
+
+test_unit = functools.partial(ends_tell, axis_name="seq")
 
 
 def per_device(inputs, out_grads, valid, doc_blocks, doc_ids, proj_in, proj_out, test_grads):
@@ -35,7 +47,7 @@
     weighted = (onehot[:, :, None] * pg[:, None, :]).reshape(slots, DOC_GRP * PROJ_OUT)
     partial_grads = jnp.dot(weighted.T, px, precision=lax.Precision.HIGHEST).reshape(DOC_GRP, FEAT)
     ndocs = DOC_GRP * lax.axis_size("dp")
-    group_grads = lax.psum(partial_grads, "seq")
+    group_grads = test_unit(partial_grads)
     doc_grads = lax.all_gather(group_grads, "dp", axis=0, tiled=True)
     gram = jnp.dot(doc_grads, doc_grads.T, precision=lax.Precision.HIGHEST)
     cross = jnp.dot(doc_grads, test_grads.astype(jnp.float32).T, precision=lax.Precision.HIGHEST)

time: 326 us -> 215 us (0.66)
  waiting for transfers between devices: 240 us -> 115 us
  starting transfers between devices: 0.08 us -> 13.6 us
    psum x1 -> x0, waiting for transfers between devices: 148 us -> none  [per_device(): group_grads = lax.psum(partial_grads, 'seq')]
    ppermute x0 -> x5, waiting for transfers between devices: none -> 18.4 us  [ends_tell(): block_now = block_now + lax.ppermute(block_now, axis_name, idx)]
    ppermute x0 -> x5, starting transfers between devices: none -> 13.5 us  [ends_tell(): block_now = block_now + lax.ppermute(block_now, axis_name, idx)]
    all_gather x1, waiting for transfers between devices: 47.1 us -> 50.7 us  [per_device(): doc_grads = lax.all_gather(group_grads, 'dp', axis=0, tiled=True)]
  transfers between devices with their start and end apart: 3 -> 7, of which waited for: 3 -> 7; matrix products, arithmetic and copies ran while one was open for 1% -> 1% of each run, Pallas kernels for 0% -> 0%
where the time goes in v1:
time: 215 us; the launch traced here: 214 us
  waiting for transfers between devices  115 us (53%)
  blocking collectives  41.4 us (19%)
  other arithmetic  14.4 us (7%)
  between operations  14.3 us (7%)
  starting transfers between devices  13.6 us (6%)
  matrix products  8.01 us (4%)
  local copies, waits for them, and re-layouts  8 us (4%)
    all_gather x1, waiting for transfers between devices, per_device(): doc_grads = lax.all_gather(group_grads, 'dp', axis=0, tiled=True)  50.7 us
    all_gather x1, waiting for transfers between devices, per_device(): lax.all_gather(proj_out, 'seq', axis=0, tiled=True)  44.7 us
    all_gather x1, blocking collectives, per_device(): lax.all_gather(proj_in, 'seq', axis=0, tiled=True)  41.4 us
    ppermute x5, waiting for transfers between devices, ends_tell(): block_now = block_now + lax.ppermute(block_now, axis_name, idx)  18.4 us
    ppermute x5, starting transfers between devices, ends_tell(): block_now = block_now + lax.ppermute(block_now, axis_name, idx)  13.5 us
    another operation x3, other arithmetic, per_device(): factor = jnp.linalg.cholesky(matrix)  6.52 us
    another operation x2, other arithmetic, per_device(): lax.linalg.triangular_solve(factor, middle, left_side=True, lower=True, t...  5.55 us
    unnamed x8, local copies, waits for them, and re-layouts  4.99 us
  transfers between devices with their start and end apart: 7, of which 7 were waited for; matrix products, arithmetic and copies ran while one was open for 1% of the time, Pallas kernels for 0%

profile of v1, /device:TPU:1, one launch (start us, length us, event | category | flops | bytes accessed | tf_op | source)
XLA Modules:
  0.0 214.1 jit_solution(16331824302549956291)
XLA Ops:
  6.5 0.0 copy-start
  6.5 0.0 all-gather.5.cloned.1.call-start
  6.5 0.7 all-gather.5.cloned.1.call-update
  7.3 0.0 all-gather.7.cloned.1.call-start
  7.3 0.8 reduce-window.8
  8.1 0.1 convert_reduce_fusion
  8.2 41.4 %all_gather.10 = bf16[4096,64]{0,1:T(8,128)(2,1)S(1)} all-gather(bf16[128,64]{0,1:T(8,128)(2,1)} %param.13), channel_id=1, replica_groups=mesh['dp'=16,'seq'=32] {'seq'}, dimensions={0}, use_global_device_ids=true | all-gather | bytes 540672 | tf_op jit(solution)/shard_map/all_gather | solution.py:31
  49.6 0.7 compare_bitcast_fusion
  50.3 0.0 copy-done
  50.3 0.5 fusion.2
  50.8 44.7 %all-gather.5.cloned.1.call-done = bf16[32,448,64]{1,2,0:T(8,128)(2,1)} async-done(((bf16[1,448,64]{1,2,0:T(8,128)(2,1)}), bf16[32,448,64]{1,2,0:T(8,128)(2,1)}) %all-gather.5.cloned.1.call-update) | async-done | bytes 1835024 | tf_op jit(solution)/shard_map/all_gather | solution.py:37
  95.6 2.8 %copy.20 = bf16[32,448,64]{1,0,2:T(8,128)(2,1)S(1)} copy(bf16[32,448,64]{1,2,0:T(8,128)(2,1)} %all-gather.5.cloned.1.call-done) | data formatting | bytes 3670016 | tf_op jit(solution)/shard_map/all_gather | solution.py:37
  98.3 3.4 %reshape.113 = bf16[14336,64]{0,1:T(8,128)(2,1)} reshape(bf16[32,448,64]{1,0,2:T(8,128)(2,1)S(1)} %copy.20) | data formatting | bytes 3670016
  101.7 4.0 %fusion = f32[128,64]{0,1:T(8,128)S(1)} fusion(bf16[14336,64]{0,1:T(8,128)(2,1)} %reshape.113, bf16[1,128,14336]{2,1,0:T(8,128)(2,1)} %param.9), kind=kOutput, calls=%fused_computation | convolution fusion | flops 234881024 | bytes 5537792 | tf_op jit(solution)/shard_map/dot_general | solution.py:35
  105.7 0.3 fusion.15
  106.0 0.1 reshape.111
  106.1 2.0 collective-permute-start
  108.1 3.0 %collective-permute-done = f32[4,4096]{1,0:T(4,128)S(1)} collective-permute-done((f32[4,4096]{1,0:T(4,128)S(1)}, f32[4,4096]{1,0:T(4,128)S(1)}, u32[]{:S(2)}, u32[]{:S(2)}) %collective-permute-start) | collective-permute-done | bytes 65568 | tf_op jit(solution)/shard_map/ppermute | solution.py:17
  111.1 2.9 %collective-permute-start.1 = (f32[4,4096]{1,0:T(4,128)S(1)}, f32[4,4096]{1,0:T(4,128)S(1)}, u32[]{:S(2)}, u32[]{:S(2)}) collective-permute-start(f32[4,4096]{1,0:T(4,128)S(1)} %add.51), channel_id=1, source_target_pairs={{0,2},{1,3},{2,0},{3,1},{4,6},{5,7},{6,4},{7,5},{8,10},{9,11},{10,... | collective-permute-start | bytes 196616 | tf_op jit(solution)/shard_map/ppermute | solution.py:17
  114.0 3.5 %collective-permute-done.1 = f32[4,4096]{1,0:T(4,128)S(1)} collective-permute-done((f32[4,4096]{1,0:T(4,128)S(1)}, f32[4,4096]{1,0:T(4,128)S(1)}, u32[]{:S(2)}, u32[]{:S(2)}) %collective-permute-start.1) | collective-permute-done | bytes 65568 | tf_op jit(solution)/shard_map/ppermute | solution.py:17
  117.6 3.4 %collective-permute-start.2 = (f32[4,4096]{1,0:T(4,128)S(1)}, f32[4,4096]{1,0:T(4,128)S(1)}, u32[]{:S(2)}, u32[]{:S(2)}) collective-permute-start(f32[4,4096]{1,0:T(4,128)S(1)} %add.52), channel_id=1, source_target_pairs={{0,4},{1,5},{2,6},{3,7},{4,0},{5,1},{6,2},{7,3},{8,12},{9,13},{10,... | collective-permute-start | bytes 196616 | tf_op jit(solution)/shard_map/ppermute | solution.py:17
  121.0 5.5 %collective-permute-done.2 = f32[4,4096]{1,0:T(4,128)S(1)} collective-permute-done((f32[4,4096]{1,0:T(4,128)S(1)}, f32[4,4096]{1,0:T(4,128)S(1)}, u32[]{:S(2)}, u32[]{:S(2)}) %collective-permute-start.2) | collective-permute-done | bytes 65568 | tf_op jit(solution)/shard_map/ppermute | solution.py:17
  126.5 1.9 collective-permute-start.3
  128.5 3.1 %collective-permute-done.3 = f32[4,4096]{1,0:T(4,128)S(1)} collective-permute-done((f32[4,4096]{1,0:T(4,128)S(1)}, f32[4,4096]{1,0:T(4,128)S(1)}, u32[]{:S(2)}, u32[]{:S(2)}) %collective-permute-start.3) | collective-permute-done | bytes 65568 | tf_op jit(solution)/shard_map/ppermute | solution.py:17
  131.6 3.2 %collective-permute-start.4 = (f32[4,4096]{1,0:T(4,128)S(1)}, f32[4,4096]{1,0:T(4,128)S(1)}, u32[]{:S(2)}, u32[]{:S(2)}) collective-permute-start(f32[4,4096]{1,0:T(4,128)S(1)} %add.54), channel_id=1, source_target_pairs={{0,16},{1,17},{2,18},{3,19},{4,20},{5,21},{6,22},{7,23},{8,24},{9,... | collective-permute-start | bytes 196616 | tf_op jit(solution)/shard_map/ppermute | solution.py:17
  134.8 3.3 %collective-permute-done.4 = f32[4,4096]{1,0:T(4,128)S(1)} collective-permute-done((f32[4,4096]{1,0:T(4,128)S(1)}, f32[4,4096]{1,0:T(4,128)S(1)}, u32[]{:S(2)}, u32[]{:S(2)}) %collective-permute-start.4) | collective-permute-done | bytes 65568 | tf_op jit(solution)/shard_map/ppermute | solution.py:17
  138.1 0.6 add_bitcast_fusion
  138.7 0.0 all-gather.7.cloned.1.call-update
  138.8 0.0 copy-start.1
  138.8 50.7 %all-gather.7.cloned.1.call-done = f32[16,4,4096]{2,1,0:T(4,128)} async-done(((f32[1,4,4096]{2,1,0:T(4,128)}), f32[16,4,4096]{2,1,0:T(4,128)}) %all-gather.7.cloned.1.call-update) | async-done | bytes 1048592 | tf_op jit(solution)/shard_map/all_gather | solution.py:51
  189.5 1.6 reshape.115
  191.0 0.0 copy-start.2
  191.1 1.6 select_reduce_fusion.1
  192.6 0.1 copy.22
  192.7 0.1 copy.23
  193.5 5.8 %cholesky.17 = f32[64,64]{1,0:T(8,128)S(1)} custom-call(f32[64,64]{1,0:T(8,128)S(1)} %fusion.10), custom_call_target="Cholesky" | custom-call | tf_op jit(solution)/shard_map/jit(cholesky)/cholesky | solution.py:56
  199.4 0.6 compare_reduce_fusion
  200.0 0.7 fusion.4
  200.7 4.9 %custom-call.8 = f32[1,64,64]{1,2,0:T(8,128)S(1)} custom-call(f32[1,64,64]{2,1,0:T(8,128)S(1)} %fusion.4), custom_call_target="InvertDiagBlocksLowerTriangular" | custom-call | tf_op jit(solution)/shard_map/triangular_solve | solution.py:58
  205.6 0.0 copy-done.1
  205.6 0.6 fusion.16
  206.2 0.1 fusion.7
  206.3 0.2 fusion.5
  206.5 0.0 copy-done.2
  206.5 0.8 fusion.11
  (10 shorter events, 0.2 us)
Async XLA Ops:
  6.5 43.8 %copy-start = (bf16[1,128,4096]{2,1,0:T(8,128)(2,1)S(1)}, bf16[1,128,4096]{2,1,0:T(8,128)(2,1)}, u32[]{:S(2)}) copy-start(bf16[1,128,4096]{2,1,0:T(8,128)(2,1)} %param.8) | copy-start | bytes 3145732
  6.5 89.0 %all-gather.5.cloned.1.call-start = ((), (), s32[]{:S(2)}) async-start(), calls=%async_computation | async-start | bytes 2162688 | tf_op jit(solution)/shard_map/all_gather | solution.py:37
  7.3 182.2 %all-gather.7.cloned.1.call-start = ((), (), s32[]{:S(2)}) async-start(), calls=%async_computation.1 | async-start | bytes 1114112 | tf_op jit(solution)/shard_map/all_gather | solution.py:51
  106.1 5.0 %collective-permute-start = (f32[4,4096]{1,0:T(4,128)S(1)}, f32[4,4096]{1,0:T(4,128)S(1)}, u32[]{:S(2)}, u32[]{:S(2)}) collective-permute-start(f32[4,4096]{1,0:T(4,128)S(1)} %reshape.111), channel_id=1, source_target_pairs={{0,1},{1,0},{2,3},{3,2},{4,5},{5,4},{6,7},{7,6},{8,9},{9,8},{10,11... | collective-permute-start | bytes 196616 | tf_op jit(solution)/shard_map/ppermute | solution.py:17
  111.1 6.5 %collective-permute-start.1 = (f32[4,4096]{1,0:T(4,128)S(1)}, f32[4,4096]{1,0:T(4,128)S(1)}, u32[]{:S(2)}, u32[]{:S(2)}) collective-permute-start(f32[4,4096]{1,0:T(4,128)S(1)} %add.51), channel_id=1, source_target_pairs={{0,2},{1,3},{2,0},{3,1},{4,6},{5,7},{6,4},{7,5},{8,10},{9,11},{10,... | collective-permute-start | bytes 196616 | tf_op jit(solution)/shard_map/ppermute | solution.py:17
  117.6 8.9 %collective-permute-start.2 = (f32[4,4096]{1,0:T(4,128)S(1)}, f32[4,4096]{1,0:T(4,128)S(1)}, u32[]{:S(2)}, u32[]{:S(2)}) collective-permute-start(f32[4,4096]{1,0:T(4,128)S(1)} %add.52), channel_id=1, source_target_pairs={{0,4},{1,5},{2,6},{3,7},{4,0},{5,1},{6,2},{7,3},{8,12},{9,13},{10,... | collective-permute-start | bytes 196616 | tf_op jit(solution)/shard_map/ppermute | solution.py:17
  126.5 5.0 %collective-permute-start.3 = (f32[4,4096]{1,0:T(4,128)S(1)}, f32[4,4096]{1,0:T(4,128)S(1)}, u32[]{:S(2)}, u32[]{:S(2)}) collective-permute-start(f32[4,4096]{1,0:T(4,128)S(1)} %add.53), channel_id=1, source_target_pairs={{0,8},{1,9},{2,10},{3,11},{4,12},{5,13},{6,14},{7,15},{8,0},{9,1},... | collective-permute-start | bytes 196616 | tf_op jit(solution)/shard_map/ppermute | solution.py:17
  131.6 6.5 %collective-permute-start.4 = (f32[4,4096]{1,0:T(4,128)S(1)}, f32[4,4096]{1,0:T(4,128)S(1)}, u32[]{:S(2)}, u32[]{:S(2)}) collective-permute-start(f32[4,4096]{1,0:T(4,128)S(1)} %add.54), channel_id=1, source_target_pairs={{0,16},{1,17},{2,18},{3,19},{4,20},{5,21},{6,22},{7,23},{8,24},{9,... | collective-permute-start | bytes 196616 | tf_op jit(solution)/shard_map/ppermute | solution.py:17
  138.8 66.8 %copy-start.1 = (bf16[32,4096]{1,0:T(8,128)(2,1)S(1)}, bf16[32,4096]{1,0:T(8,128)(2,1)}, u32[]{:S(2)}) copy-start(bf16[32,4096]{1,0:T(8,128)(2,1)} %param.15) | copy-start | bytes 786436
  191.0 15.5 %copy-start.2 = (s32[64]{0:T(128)S(1)}, s32[64]{0:T(128)}, u32[]{:S(2)}) copy-start(s32[64]{0:T(128)} %param.12) | copy-start | bytes 772
Sparse Core Ops, SparseCore 0:
  10.5 84.9 all-gather.4
  138.9 50.5 all-gather.6
